TPU v7x, 128 devices: a whole 4x4x4 slice. The times are simulated.
128 devices in a mesh: grp: 4 (over x_lo, core), mz: 32 (over y, x_hi, z).
Axes of the slice: x: 4 (x_hi: 2, x_lo: 2; x = x_hi * 2 + x_lo), y: 4, z: 4, core: 2. Of those that a mesh axis runs over, the one named last changes fastest.
Arguments:
- intensities: float32 [512, 8, 131072], P('grp', None, 'mz'), as said below
- sample_start: float32 [512, 256], P('grp'), as said below
- scan_start: float32 [8, 256], replicated, as said below
- mass_start: float32 [131072, 256], P('mz'), as said below
Outputs:
- sample_factor: float32 [512, 256], P('grp')
- scan_factor: float32 [8, 256], replicated
- mass_factor: float32 [131072, 256], P('mz')
Inputs may be any that keep to these rules, and one draw needn't show every extreme that they name: Measured intensities of the cohort. `sample_start`: a starting estimate of the sample factor. `scan_start`: a starting estimate of the scan factor. `mass_start`: a starting estimate of the m/z factor.
All inputs are finite; a program needn't handle non-finite values.
Results may differ from a plain program's by a relative error of at most 0.0001.
Values sent between devices are 32-bit elements; how exact they have to be, the bound alone decides.
A program may use at most 128 MiB of HBM per device.

v0:
```python
import jax
import jax.numpy as jnp
from jax import lax
from jax.sharding import PartitionSpec as P

STEPS = 2
precise = lax.Precision.HIGHEST


def frobenius(gram):
    return jnp.sqrt(jnp.sum(gram * gram) + 1e-12)


def gram_of(factor):
    return jnp.dot(factor.T, factor, precision=precise, preferred_element_type=jnp.float32)


def descend(factor, hessian, drive):
    product = jnp.dot(factor, hessian, precision=precise, preferred_element_type=jnp.float32)
    return factor - (product - drive) / frobenius(hessian)


def local(intensities, sample_start, scan_start, mass_start):
    factor_a = sample_start
    factor_b = scan_start
    factor_c = mass_start
    samples_here = intensities.shape[0]
    scans_here = intensities.shape[1]
    bins_here = intensities.shape[2]
    rank_width = factor_a.shape[1]
    unfolded = intensities.reshape(samples_here * scans_here, bins_here)
    for iteration in range(STEPS):
        gram_a = lax.psum(gram_of(factor_a), "grp")
        gram_b = gram_of(factor_b)
        gram_c = lax.psum(gram_of(factor_c), "mz")
        contracted = jnp.einsum("ijk,kr->ijr", intensities, factor_c, precision=precise)
        drive_a = lax.psum(jnp.einsum("ijr,jr->ir", contracted, factor_b, precision=precise), "mz")
        drive_b = lax.psum(
            jnp.einsum("ijr,ir->jr", contracted, factor_a, precision=precise), ("grp", "mz")
        )
        khatri_rao = (factor_a[:, None, :] * factor_b[None, :, :]).reshape(
            samples_here * scans_here, rank_width
        )
        hessian_a = gram_b * gram_c
        hessian_b = gram_a * gram_c
        hessian_c = gram_a * gram_b
        partial_c = lax.dot_general(
            unfolded,
            khatri_rao,
            (((0,), (0,)), ((), ())),
            precision=precise,
            preferred_element_type=jnp.float32,
        )
        drive_c = lax.psum(partial_c, "grp")
        new_c = descend(factor_c, hessian_c, drive_c)
        new_a = descend(factor_a, hessian_a, drive_a)
        new_b = descend(factor_b, hessian_b, drive_b)
        factor_a, factor_b, factor_c = (new_a, new_b, new_c)
    return (factor_a, factor_b, factor_c)


def solution(mesh):
    placed = (P("grp", None, "mz"), P("grp", None), P(), P("mz", None))
    return jax.shard_map(
        local,
        mesh=mesh,
        in_specs=placed,
        out_specs=(P("grp", None), P(), P("mz", None)),
        check_vma=False,
    )
```

profile of v0, /device:TPU:1, one launch (start us, length us, event | category | flops | bytes accessed | tf_op | source)
XLA Modules:
  0.0 1056.7 jit_solution(8836801280862759096)
XLA Ops:
  7.2 0.0 all-reduce.12.cloned.1.call-start
  7.2 0.0 copy-start
  7.2 11.1 %fusion.53 = f32[256,256]{1,0:T(8,128)} fusion(f32[4096,256]{1,0:T(8,128)} %param.7), kind=kOutput, calls=%fused_computation.59 | convolution fusion | flops 3221225472 | bytes 4456448 | tf_op jit(solution)/shard_map/dot_general | solution.py:15
  18.3 0.0 copy-done
  18.3 0.0 copy-start.6
  18.3 0.0 copy-start.2
  18.3 16.7 %fusion.18 = f32[128,8,256]{2,1,0:T(8,128)S(1)} fusion(f32[128,8,4096]{2,1,0:T(8,128)} %param.4, f32[4096,256]{1,0:T(8,128)S(1)} %copy-done), kind=kOutput, calls=%fused_computation.16 | convolution fusion | flops 12884901888 | bytes 22020096 | tf_op jit(solution)/shard_map/ijk,kr->ijr/dot_general | solution.py:36
  35.0 0.0 copy-done.6
  35.0 0.3 fusion.36
  35.3 0.8 copy.26
  36.1 0.0 all-reduce.12.cloned.1.call-update
  36.1 0.3 all-reduce.16.cloned.1.call-start
  36.4 0.0 copy-done.2
  36.4 0.1 copy.8
  36.5 28.8 %fusion.7 = f32[4096,256]{0,1:T(8,128)} fusion(f32[128,8,4096]{2,1,0:T(8,128)} %param.4, f32[8,256]{1,0:T(8,128)S(1)} %copy-done.6, f32[128,256]{0,1:T(8,128)S(1)} %copy.8), kind=kOutput, calls=%fused_computation.9 | convolution fusion | flops 12885164032 | bytes 21110784 | tf_op jit(solution)/shard_map/dot_general | solution.py:47
  65.3 1.1 fusion.54
  66.4 0.0 all-reduce.16.cloned.1.call-update
  66.4 0.4 all-reduce.10.cloned.1.call-start
  66.9 5.7 copy.11
  72.6 0.3 fusion.35
  72.9 286.1 %all-reduce.12.cloned.1.call-done = (f32[128,256]{0,1:T(8,128)}, f32[256,256]{1,0:T(8,128)}) async-done(((f32[128,256]{0,1:T(8,128)}, f32[256,256]{1,0:T(8,128)}), (f32[128,256]{0,1:T(8,128)}, f32[256,256]{1,0:T(8,128)})) %all-reduce.12.cloned.1.call-update) | async-done | bytes 393232 | tf_op jit(solution)/shard_map/psum | solution.py:37
  359.0 115.0 %all-reduce.16.cloned.1.call-done = (f32[256,256]{1,0:T(8,128)}, f32[4096,256]{0,1:T(8,128)}) async-done(((f32[256,256]{1,0:T(8,128)}, f32[4096,256]{0,1:T(8,128)}), (f32[256,256]{1,0:T(8,128)}, f32[4096,256]{0,1:T(8,128)})) %all-reduce.16.cloned.1.call-update) | async-done | bytes 4456464 | tf_op jit(solution)/shard_map/psum | solution.py:33
  474.0 2.1 multiply_reduce_fusion.3
  476.8 11.9 %fusion.14 = f32[4096,256]{0,1:T(8,128)S(1)} fusion(f32[4096,256]{0,1:T(8,128)} %copy.11, f32[4096,256]{0,1:T(8,128)} %get-tuple-element.21, f32[4096,256]{1,0:T(8,128)} %param.7, f32[]{:T(128)S(6)} %sqrt.20, f32[256,256]{1,0:T(8,128)} %get-tuple-element.20, f32[256,256]{1,0:T(8,128)S(1)} %get-tuple-element.22), kind=kOutput, calls=%fused_computation.12 | convolution fusion | flops 3224436736 | bytes 17301508 | tf_op jit(solution)/shard_map/dot_general | solution.py:19
  488.7 0.0 copy-start.1
  488.8 4.3 fusion.55
  493.0 0.0 copy-done.1
  493.0 0.0 copy-start.5
  493.0 0.0 copy-start.8
  493.0 0.0 copy-start.3
  493.0 28.1 %fusion.20 = f32[128,8,256]{0,2,1:T(8,128)S(1)} fusion(f32[128,8,4096]{2,1,0:T(8,128)} %param.4, f32[4096,256]{0,1:T(8,128)S(1)} %fusion.14), kind=kOutput, calls=%fused_computation.18 | convolution fusion | flops 12884901888 | bytes 22020096 | tf_op jit(solution)/shard_map/ijk,kr->ijr/dot_general | solution.py:36
  522.5 0.0 copy-done.5
  522.5 0.0 copy-done.8
  522.5 0.6 fusion.29
  523.1 2.3 fusion.39
  525.4 0.1 copy.38
  525.5 66.3 %all-reduce = (f32[8,256]{1,0:T(8,128)S(1)}, f32[8,256]{1,0:T(8,128)S(1)}) all-reduce(f32[8,256]{1,0:T(8,128)S(1)} %bitcast.90, f32[8,256]{1,0:T(8,128)S(1)} %bitcast.91), channel_id=1, replica_groups=mesh['grp'=4,'mz'=32] {'grp','mz'}, use_global_device_ids=true, to_apply=%region_4.0 | all-reduce | flops 4096 | bytes 32768 | tf_op jit(solution)/shard_map/psum | solution.py:38
  591.7 0.0 copy-done.3
  591.7 0.2 fusion.34
  592.0 0.1 copy.34
  592.1 3.0 fusion.41
  595.1 0.0 all-reduce.10.cloned.1.call-update
  595.1 0.0 all-reduce.14.cloned.1.call-start
  595.2 29.0 %fusion.10 = f32[4096,256]{0,1:T(8,128)} fusion(f32[128,8,4096]{2,1,0:T(8,128)} %param.4, f32[8,256]{1,0:T(8,128)S(1)} %fusion.34, f32[128,256]{0,1:T(8,128)S(1)} %fusion.29), kind=kOutput, calls=%fused_computation.10 | convolution fusion | flops 12885164032 | bytes 21110784 | tf_op jit(solution)/shard_map/dot_general | solution.py:47
  624.2 1.1 fusion.56
  625.3 0.0 all-reduce.14.cloned.1.call-update
  625.3 285.8 %all-reduce.10.cloned.1.call-done = (f32[128,256]{0,1:T(8,128)}, f32[256,256]{1,0:T(8,128)}) async-done(((f32[128,256]{0,1:T(8,128)}, f32[256,256]{1,0:T(8,128)}), (f32[128,256]{0,1:T(8,128)}, f32[256,256]{1,0:T(8,128)})) %all-reduce.10.cloned.1.call-update) | async-done | bytes 393232 | tf_op jit(solution)/shard_map/psum | solution.py:37
  911.1 114.7 %all-reduce.14.cloned.1.call-done = (f32[256,256]{1,0:T(8,128)}, f32[4096,256]{0,1:T(8,128)}) async-done(((f32[256,256]{1,0:T(8,128)}, f32[4096,256]{0,1:T(8,128)}), (f32[256,256]{1,0:T(8,128)}, f32[4096,256]{0,1:T(8,128)})) %all-reduce.14.cloned.1.call-update) | async-done | bytes 4456464 | tf_op jit(solution)/shard_map/psum | solution.py:33
  1025.8 2.1 multiply_reduce_fusion
  1029.9 1.6 fusion.26
  1031.5 0.8 copy.16
  1032.3 11.0 %fusion.16 = f32[4096,256]{0,1:T(8,128)} fusion(f32[4096,256]{0,1:T(8,128)} %copy-done.1, f32[4096,256]{0,1:T(8,128)} %get-tuple-element.19, f32[]{:T(128)S(6)} %sqrt.23, f32[256,256]{1,0:T(8,128)} %get-tuple-element.18, f32[256,256]{1,0:T(8,128)S(1)} %get-tuple-element.23), kind=kOutput, calls=%fused_computation.14 | convolution fusion | flops 3224436736 | bytes 13107204 | tf_op jit(solution)/shard_map/dot_general | solution.py:19
  1043.3 0.0 copy-start.4
  1043.3 0.0 copy-start.7
  1043.3 5.7 copy.17
  1048.9 0.0 copy-done.4
  1048.9 0.0 copy-done.7
  1048.9 0.8 fusion.31
Async XLA Ops:
  7.2 351.9 %all-reduce.12.cloned.1.call-start = ((), (), s32[]{:S(2)}) async-start(), calls=%async_computation.1 | async-start | bytes 786432 | tf_op jit(solution)/shard_map/psum | solution.py:37
  7.2 11.1 %copy-start = (f32[4096,256]{1,0:T(8,128)S(1)}, f32[4096,256]{1,0:T(8,128)}, u32[]{:S(2)}) copy-start(f32[4096,256]{1,0:T(8,128)} %param.7) | copy-start | bytes 12582916
  18.3 16.7 %copy-start.6 = (f32[8,256]{1,0:T(8,128)S(1)}, f32[8,256]{1,0:T(8,128)}, u32[]{:S(2)}) copy-start(f32[8,256]{1,0:T(8,128)} %param.6) | copy-start | bytes 24580
  18.3 18.1 %copy-start.2 = (f32[128,256]{1,0:T(8,128)S(1)}, f32[128,256]{1,0:T(8,128)}, u32[]{:S(2)}) copy-start(f32[128,256]{1,0:T(8,128)} %param.5) | copy-start | bytes 393220
  36.1 437.9 %all-reduce.16.cloned.1.call-start = ((), (), s32[]{:S(2)}) async-start(), calls=%async_computation.3 | async-start | bytes 8912896 | tf_op jit(solution)/shard_map/psum | solution.py:33
  66.4 844.6 %all-reduce.10.cloned.1.call-start = ((), (), s32[]{:S(2)}) async-start(), calls=%async_computation | async-start | bytes 786432 | tf_op jit(solution)/shard_map/psum | solution.py:37
  488.7 4.3 copy-start.1
  493.0 29.5 %copy-start.5 = (f32[256,256]{1,0:T(8,128)S(1)}, f32[256,256]{1,0:T(8,128)}, u32[]{:S(2)}) copy-start(f32[256,256]{1,0:T(8,128)} %get-tuple-element.17) | copy-start | bytes 786436
  493.0 29.5 %copy-start.8 = (f32[128,256]{0,1:T(8,128)S(1)}, f32[128,256]{0,1:T(8,128)}, u32[]{:S(2)}) copy-start(f32[128,256]{0,1:T(8,128)} %get-tuple-element.16) | copy-start | bytes 393220
  493.0 98.7 %copy-start.3 = (f32[256,256]{1,0:T(8,128)S(1)}, f32[256,256]{1,0:T(8,128)}, u32[]{:S(2)}) copy-start(f32[256,256]{1,0:T(8,128)} %get-tuple-element.20) | copy-start | bytes 786436
  595.1 430.6 %all-reduce.14.cloned.1.call-start = ((), (), s32[]{:S(2)}) async-start(), calls=%async_computation.2 | async-start | bytes 8912896 | tf_op jit(solution)/shard_map/psum | solution.py:33
  1043.3 5.7 copy-start.4
  1043.3 5.7 copy-start.7
Sparse Core Ops, SparseCore 0:
  36.2 322.7 all-reduce.11
  362.4 111.6 all-reduce.15
  595.3 315.7 all-reduce.9
  914.1 111.6 all-reduce.13
where the time goes:
time: 1060 us
  waiting for transfers between devices  802 us (76%)
  matrix products  156 us (15%)
  blocking collectives  66.3 us (6%)
  between operations  18.5 us (2%)
  local copies, waits for them, and re-layouts  13.2 us (1%)
    psum x2, waiting for transfers between devices, local(): lax.psum(jnp.einsum('ijr,jr->ir', contracted, factor_b, precision=precise...  572 us
    psum x2, waiting for transfers between devices, local(): gram_a = lax.psum(gram_of(factor_a), 'grp')  230 us
    psum x1, blocking collectives, local(): lax.psum(jnp.einsum('ijr,ir->jr', contracted, factor_a, precision=precise...  66.3 us
    dot_general x2, matrix products, local(): lax.dot_general(unfolded, khatri_rao, (((0,), (0,)), ((), ())), precision...  57.8 us
    dot_general x2, matrix products, local(): jnp.einsum('ijk,kr->ijr', intensities, factor_c, precision=precise)  44.8 us
    dot_general x6, matrix products, descend(): jnp.dot(factor, hessian, precision=precise, preferred_element_type=jnp.fl...  26.2 us
    dot_general x6, matrix products, gram_of(): jnp.dot(factor.T, factor, precision=precise, preferred_element_type=jnp.f...  21.7 us
  transfers between devices with their start and end apart: 4, of which 4 were waited for; matrix products, arithmetic and copies ran while one was open for 6% of the time, Pallas kernels for 0%

commit v1 on v0

--- a/solution.py
+++ b/solution.py
@@ -36,7 +36,7 @@
         contracted = jnp.einsum("ijk,kr->ijr", intensities, factor_c, precision=precise)
         drive_a = lax.psum(jnp.einsum("ijr,jr->ir", contracted, factor_b, precision=precise), "mz")
         drive_b = lax.psum(
-            jnp.einsum("ijr,ir->jr", contracted, factor_a, precision=precise), ("grp", "mz")
+            lax.psum(jnp.einsum("ijr,ir->jr", contracted, factor_a, precision=precise), "mz"), "grp"
         )
         khatri_rao = (factor_a[:, None, :] * factor_b[None, :, :]).reshape(
             samples_here * scans_here, rank_width

time: 1060 us -> 1190 us (1.12)
  blocking collectives: 66.3 us -> 192 us
    psum x1, blocking collectives: 66.3 us -> 156 us  [local(): lax.psum(jnp.einsum('ijr,ir->jr', contracted, factor_a, precision=precise...]
    psum x0 -> x1, blocking collectives: none -> 35.9 us  [local(): lax.psum(lax.psum(jnp.einsum('ijr,ir->jr', contracted, factor_a, precisio...]
where the time goes in v1:
time: 1190 us; the launch traced here: 1180 us
  waiting for transfers between devices  800 us (67%)
  blocking collectives  192 us (16%)
  matrix products  156 us (13%)
  between operations  18.5 us (2%)
  local copies, waits for them, and re-layouts  13.2 us (1%)
    psum x2, waiting for transfers between devices, local(): lax.psum(jnp.einsum('ijr,jr->ir', contracted, factor_b, precision=precise...  570 us
    psum x2, waiting for transfers between devices, local(): gram_a = lax.psum(gram_of(factor_a), 'grp')  230 us
    psum x1, blocking collectives, local(): lax.psum(jnp.einsum('ijr,ir->jr', contracted, factor_a, precision=precise...  156 us
    dot_general x2, matrix products, local(): lax.dot_general(unfolded, khatri_rao, (((0,), (0,)), ((), ())), precision...  57.8 us
    dot_general x2, matrix products, local(): jnp.einsum('ijk,kr->ijr', intensities, factor_c, precision=precise)  44.8 us
    psum x1, blocking collectives, local(): lax.psum(lax.psum(jnp.einsum('ijr,ir->jr', contracted, factor_a, precisio...  35.9 us
    dot_general x6, matrix products, descend(): jnp.dot(factor, hessian, precision=precise, preferred_element_type=jnp.fl...  26.2 us
  transfers between devices with their start and end apart: 4, of which 4 were waited for; matrix products, arithmetic and copies ran while one was open for 6% of the time, Pallas kernels for 0%

profile of v1, /device:TPU:1, one launch (start us, length us, event | category | flops | bytes accessed | tf_op | source)
XLA Modules:
  0.0 1180.7 jit_solution(4784915144424831025)
XLA Ops:
  7.2 0.0 all-reduce.13.cloned.1.call-start
  7.2 0.0 copy-start
  7.2 11.1 fusion.53
  18.3 0.0 copy-done
  18.3 0.0 copy-start.6
  18.3 0.0 copy-start.2
  18.3 16.7 %fusion.18 = f32[128,8,256]{2,1,0:T(8,128)S(1)} fusion(f32[128,8,4096]{2,1,0:T(8,128)} %param.4, f32[4096,256]{1,0:T(8,128)S(1)} %copy-done), kind=kOutput, calls=%fused_computation.16 | convolution fusion | flops 12884901888 | bytes 22020096 | tf_op jit(solution)/shard_map/ijk,kr->ijr/dot_general | solution.py:36
  35.0 0.0 copy-done.6
  35.0 0.3 fusion.36
  35.3 0.8 copy.26
  36.1 0.0 all-reduce.13.cloned.1.call-update
  36.1 0.3 all-reduce.17.cloned.1.call-start
  36.4 0.0 copy-done.2
  36.4 0.1 copy.8
  36.5 28.8 %fusion.7 = f32[4096,256]{0,1:T(8,128)} fusion(f32[128,8,4096]{2,1,0:T(8,128)} %param.4, f32[8,256]{1,0:T(8,128)S(1)} %copy-done.6, f32[128,256]{0,1:T(8,128)S(1)} %copy.8), kind=kOutput, calls=%fused_computation.9 | convolution fusion | flops 12885164032 | bytes 21110784 | tf_op jit(solution)/shard_map/dot_general | solution.py:47
  65.3 1.1 fusion.54
  66.4 0.0 all-reduce.17.cloned.1.call-update
  66.4 0.4 all-reduce.11.cloned.1.call-start
  66.9 5.7 copy.11
  72.6 0.3 fusion.35
  72.9 286.1 %all-reduce.13.cloned.1.call-done = (f32[128,256]{0,1:T(8,128)}, f32[256,256]{1,0:T(8,128)}) async-done(((f32[128,256]{0,1:T(8,128)}, f32[256,256]{1,0:T(8,128)}), (f32[128,256]{0,1:T(8,128)}, f32[256,256]{1,0:T(8,128)})) %all-reduce.13.cloned.1.call-update) | async-done | bytes 393232 | tf_op jit(solution)/shard_map/psum | solution.py:37
  359.0 115.0 %all-reduce.17.cloned.1.call-done = (f32[256,256]{1,0:T(8,128)}, f32[4096,256]{0,1:T(8,128)}) async-done(((f32[256,256]{1,0:T(8,128)}, f32[4096,256]{0,1:T(8,128)}), (f32[256,256]{1,0:T(8,128)}, f32[4096,256]{0,1:T(8,128)})) %all-reduce.17.cloned.1.call-update) | async-done | bytes 4456464 | tf_op jit(solution)/shard_map/psum | solution.py:33
  474.0 2.1 multiply_reduce_fusion.3
  476.8 11.9 %fusion.14 = f32[4096,256]{0,1:T(8,128)S(1)} fusion(f32[4096,256]{0,1:T(8,128)} %copy.11, f32[4096,256]{0,1:T(8,128)} %get-tuple-element.23, f32[4096,256]{1,0:T(8,128)} %param.7, f32[]{:T(128)S(6)} %sqrt.20, f32[256,256]{1,0:T(8,128)} %get-tuple-element.22, f32[256,256]{1,0:T(8,128)S(1)} %get-tuple-element.24), kind=kOutput, calls=%fused_computation.12 | convolution fusion | flops 3224436736 | bytes 17301508 | tf_op jit(solution)/shard_map/dot_general | solution.py:19
  488.7 0.0 copy-start.1
  488.8 4.3 fusion.55
  493.0 0.0 copy-done.1
  493.0 0.0 copy-start.5
  493.0 0.0 copy-start.8
  493.0 0.0 copy-start.3
  493.0 28.1 %fusion.20 = f32[128,8,256]{0,2,1:T(8,128)S(1)} fusion(f32[128,8,4096]{2,1,0:T(8,128)} %param.4, f32[4096,256]{0,1:T(8,128)S(1)} %fusion.14), kind=kOutput, calls=%fused_computation.18 | convolution fusion | flops 12884901888 | bytes 22020096 | tf_op jit(solution)/shard_map/ijk,kr->ijr/dot_general | solution.py:36
  522.5 0.0 copy-done.5
  522.5 0.0 copy-done.8
  522.5 0.6 fusion.29
  523.1 2.3 fusion.39
  525.4 0.1 copy.38
  525.5 155.8 %all-reduce = (f32[8,256]{1,0:T(8,128)S(1)}, f32[8,256]{1,0:T(8,128)S(1)}) all-reduce(f32[8,256]{1,0:T(8,128)S(1)} %bitcast.90, f32[8,256]{1,0:T(8,128)S(1)} %bitcast.91), channel_id=1, replica_groups=mesh['grp'=4,'mz'=32] {'mz'}, use_global_device_ids=true, to_apply=%region_4.0 | all-reduce | flops 4096 | bytes 32768 | tf_op jit(solution)/shard_map/psum | solution.py:39
  681.3 35.9 %all-reduce.3 = (f32[8,256]{1,0:T(8,128)S(1)}, f32[8,256]{1,0:T(8,128)S(1)}) all-reduce(f32[8,256]{1,0:T(8,128)S(1)} %get-tuple-element.12, f32[8,256]{1,0:T(8,128)S(1)} %get-tuple-element.13), channel_id=1, replica_groups=mesh['grp'=4,'mz'=32] {'grp'}, use_global_device_ids=true, to_apply=%region_5.0 | all-reduce | flops 4096 | bytes 32768 | tf_op jit(solution)/shard_map/psum | solution.py:38
  717.2 0.0 copy-done.3
  717.2 0.2 fusion.34
  717.4 0.1 copy.34
  717.6 3.0 fusion.41
  720.6 0.0 all-reduce.11.cloned.1.call-update
  720.6 0.0 all-reduce.15.cloned.1.call-start
  720.6 29.0 %fusion.10 = f32[4096,256]{0,1:T(8,128)} fusion(f32[128,8,4096]{2,1,0:T(8,128)} %param.4, f32[8,256]{1,0:T(8,128)S(1)} %fusion.34, f32[128,256]{0,1:T(8,128)S(1)} %fusion.29), kind=kOutput, calls=%fused_computation.10 | convolution fusion | flops 12885164032 | bytes 21110784 | tf_op jit(solution)/shard_map/dot_general | solution.py:47
  749.7 1.1 fusion.56
  750.7 0.0 all-reduce.15.cloned.1.call-update
  750.8 284.3 %all-reduce.11.cloned.1.call-done = (f32[128,256]{0,1:T(8,128)}, f32[256,256]{1,0:T(8,128)}) async-done(((f32[128,256]{0,1:T(8,128)}, f32[256,256]{1,0:T(8,128)}), (f32[128,256]{0,1:T(8,128)}, f32[256,256]{1,0:T(8,128)})) %all-reduce.11.cloned.1.call-update) | async-done | bytes 393232 | tf_op jit(solution)/shard_map/psum | solution.py:37
  1035.1 114.7 %all-reduce.15.cloned.1.call-done = (f32[256,256]{1,0:T(8,128)}, f32[4096,256]{0,1:T(8,128)}) async-done(((f32[256,256]{1,0:T(8,128)}, f32[4096,256]{0,1:T(8,128)}), (f32[256,256]{1,0:T(8,128)}, f32[4096,256]{0,1:T(8,128)})) %all-reduce.15.cloned.1.call-update) | async-done | bytes 4456464 | tf_op jit(solution)/shard_map/psum | solution.py:33
  1149.7 2.1 multiply_reduce_fusion
  1153.9 1.6 fusion.26
  1155.5 0.8 copy.16
  1156.2 11.0 fusion.16
  1167.2 0.0 copy-start.4
  1167.2 0.0 copy-start.7
  1167.2 5.7 copy.17
  1172.9 0.0 copy-done.4
  1172.9 0.0 copy-done.7
  1172.9 0.8 fusion.31
Async XLA Ops:
  7.2 351.9 %all-reduce.13.cloned.1.call-start = ((), (), s32[]{:S(2)}) async-start(), calls=%async_computation.1 | async-start | bytes 786432 | tf_op jit(solution)/shard_map/psum | solution.py:37
  7.2 11.1 copy-start
  18.3 16.7 %copy-start.6 = (f32[8,256]{1,0:T(8,128)S(1)}, f32[8,256]{1,0:T(8,128)}, u32[]{:S(2)}) copy-start(f32[8,256]{1,0:T(8,128)} %param.6) | copy-start | bytes 24580
  18.3 18.1 %copy-start.2 = (f32[128,256]{1,0:T(8,128)S(1)}, f32[128,256]{1,0:T(8,128)}, u32[]{:S(2)}) copy-start(f32[128,256]{1,0:T(8,128)} %param.5) | copy-start | bytes 393220
  36.1 437.9 %all-reduce.17.cloned.1.call-start = ((), (), s32[]{:S(2)}) async-start(), calls=%async_computation.3 | async-start | bytes 8912896 | tf_op jit(solution)/shard_map/psum | solution.py:33
  66.4 968.6 %all-reduce.11.cloned.1.call-start = ((), (), s32[]{:S(2)}) async-start(), calls=%async_computation | async-start | bytes 786432 | tf_op jit(solution)/shard_map/psum | solution.py:37
  488.7 4.3 copy-start.1
  493.0 29.5 %copy-start.5 = (f32[256,256]{1,0:T(8,128)S(1)}, f32[256,256]{1,0:T(8,128)}, u32[]{:S(2)}) copy-start(f32[256,256]{1,0:T(8,128)} %get-tuple-element.17) | copy-start | bytes 786436
  493.0 29.5 %copy-start.8 = (f32[128,256]{0,1:T(8,128)S(1)}, f32[128,256]{0,1:T(8,128)}, u32[]{:S(2)}) copy-start(f32[128,256]{0,1:T(8,128)} %get-tuple-element.16) | copy-start | bytes 393220
  493.0 224.1 %copy-start.3 = (f32[256,256]{1,0:T(8,128)S(1)}, f32[256,256]{1,0:T(8,128)}, u32[]{:S(2)}) copy-start(f32[256,256]{1,0:T(8,128)} %get-tuple-element.22) | copy-start | bytes 786436
  720.6 429.1 %all-reduce.15.cloned.1.call-start = ((), (), s32[]{:S(2)}) async-start(), calls=%async_computation.2 | async-start | bytes 8912896 | tf_op jit(solution)/shard_map/psum | solution.py:33
  1167.2 5.7 copy-start.4
  1167.2 5.7 copy-start.7
Sparse Core Ops, SparseCore 0:
  36.2 322.7 all-reduce.12
  362.4 111.6 all-reduce.16
  720.7 314.3 all-reduce.10
  1038.1 111.6 all-reduce.14
